TPU v7x, 32 devices: a whole 2x2x4 slice. The times are simulated.
32 devices in a mesh: row: 2 (over x), col: 16 (over z, y, core).
Axes of the slice: x: 2, y: 2, z: 4, core: 2. Of those that a mesh axis runs over, the one named last changes fastest.
Arguments:
- coords: float32 [64, 3, 256], P(('row', 'col')), may hold values from 0 to 8, as said below
- noise_var: float32 [64, 256], P(('row', 'col')), may hold values from 0.1 to 1
- right_side: float32 [64, 8, 256], P(('row', 'col')), may hold values from -32 to 32
- start_guess: float32 [64, 8, 256], P(('row', 'col')), may hold values from -3 to 3
- tile_pairs: int32 [2, 16, 2, 63], P('row', 'col'), may hold values from -1 to 31, as said below
Outputs:
- solution_field: float32 [64, 8, 256], P(('row', 'col'))
- residual: float32 [64, 8, 256], P(('row', 'col'))
Inputs may be any that keep to these rules, and one draw needn't show every extreme that they name: `coords`: each tile's points lie within one unit cell of the integer lattice, and distinct tiles lie in distinct cells. `tile_pairs`: each device's list holds every pair of its block whose cells differ by at most one in each coordinate, each pair once and no other; listed entries come first, then entries of -1 in both rows.
All inputs are finite; a program needn't handle non-finite values.
Results may differ from a plain program's by a relative error of at most 0.0003.
Values sent between devices are 32-bit elements; how exact they have to be, the bound alone decides.
A program may use at most 64 MiB of HBM per device.

v0:
```python
import jax
import jax.numpy as jnp
from jax import lax
from jax.sharding import PartitionSpec as P

ITERS = 3
pair_group = 2


def wendland(left_points, right_points):
    squared = jnp.zeros(
        (left_points.shape[0], left_points.shape[2], right_points.shape[2]), jnp.float32
    )
    for component in range(3):
        spacing = left_points[:, component, :, None] - right_points[:, component, None, :]
        squared = squared + spacing * spacing
    distance = jnp.sqrt(squared)
    remain = jnp.maximum(1.0 - distance, 0.0)
    return remain**4 * (4.0 * distance + 1.0)


def squares(residual):
    return lax.psum(jnp.sum(residual * residual, axis=(0, 2)), ("row", "col"))


def shards(coords, noise_var, right_side, start_guess, tile_pairs):
    row_points = lax.all_gather(coords, "col", axis=0, tiled=True)
    col_points = lax.all_gather(coords, "row", axis=0, tiled=True)
    row_count = row_points.shape[0]
    listed = tile_pairs[0, 0]
    usable = listed[0] >= 0
    sort_key = jnp.where(usable, listed[0], row_count)
    sorted_index = jnp.argsort(sort_key, stable=True)
    sorted_rows = jnp.concatenate(
        [sort_key[sorted_index], jnp.full((pair_group,), row_count, jnp.int32)]
    )
    sorted_cols = jnp.concatenate(
        [jnp.where(usable, listed[1], 0)[sorted_index], jnp.zeros((pair_group,), jnp.int32)]
    )

    def pair_range(first_row, row_number):
        first = jnp.sum(sorted_rows < first_row)
        last = jnp.sum(sorted_rows < first_row + row_number)
        return (first, last, (last - first + pair_group - 1) // pair_group)

    def group_weights(position, last):
        indices = position + jnp.arange(pair_group, dtype=jnp.int32)
        rows_group = lax.dynamic_slice_in_dim(sorted_rows, position, pair_group)
        cols_group = lax.dynamic_slice_in_dim(sorted_cols, position, pair_group)
        inside = (indices < last).astype(jnp.float32)
        safe_rows = jnp.minimum(rows_group, row_count - 1)
        weights = wendland(row_points[safe_rows], col_points[cols_group]) * inside[:, None, None]
        return (weights, safe_rows, cols_group)

    def apply_operator(vectors):
        empty = jnp.zeros((col_points.shape[0],) + vectors.shape[1:], jnp.float32)
        pieces = lax.all_gather(vectors, "col", axis=0, tiled=True)
        number = pieces.shape[0]
        first, last, turns = pair_range(jnp.int32(0), number)

        def visit(turn, running):
            weights, safe_rows, cols_group = group_weights(first + pair_group * turn, last)
            local_rows = jnp.clip(safe_rows, 0, number - 1)
            product = jnp.einsum(
                "pab,psa->psb", weights, pieces[local_rows], precision=lax.Precision.HIGHEST
            )
            return running.at[cols_group].add(product)

        gathered_sum = lax.fori_loop(0, turns, visit, empty)
        coupled = lax.psum_scatter(gathered_sum, "row", scatter_dimension=0, tiled=True)
        return coupled + noise_var[:, None, :] * vectors

    solution_field = start_guess
    residual = right_side - apply_operator(start_guess)
    direction = residual
    norm_now = squares(residual)
    for iteration in range(ITERS):
        applied = apply_operator(direction)
        step_size = norm_now / lax.psum(jnp.sum(direction * applied, axis=(0, 2)), ("row", "col"))
        solution_field = solution_field + step_size[None, :, None] * direction
        residual = residual - step_size[None, :, None] * applied
        norm_next = squares(residual)
        direction = residual + (norm_next / norm_now)[None, :, None] * direction
        norm_now = norm_next
    return (solution_field, residual)


def solution(mesh):
    placed = (
        P(("row", "col"), None, None),
        P(("row", "col"), None),
        P(("row", "col"), None, None),
        P(("row", "col"), None, None),
        P("row", "col", None, None),
    )
    return jax.shard_map(
        shards,
        mesh=mesh,
        in_specs=placed,
        out_specs=(P(("row", "col"), None, None), P(("row", "col"), None, None)),
        check_vma=False,
    )
```

profile of v0, /device:TPU:0, one launch (start us, length us, event | category | flops | bytes accessed | tf_op | source)
XLA Modules:
  0.0 646.0 jit_solution(4284149621219089081)
XLA Ops:
  8.0 2.0 sort.17
  13.5 23.5 %all_gather.19 = f32[32,3,256]{2,1,0:T(4,128)S(1)} all-gather(f32[2,3,256]{2,1,0:T(4,128)S(1)} %copy.11), channel_id=1, replica_groups=mesh['row'=2,'col'=16] {'col'}, dimensions={0}, use_global_device_ids=true | all-gather | bytes 104448 | tf_op jit(solution)/shard_map/all_gather | solution.py:27
  36.9 4.3 all_gather.20
  42.1 17.8 %all_gather.18 = f32[32,8,256]{2,1,0:T(8,128)S(1)} all-gather(f32[2,8,256]{2,1,0:T(8,128)S(1)} %copy-done.5), channel_id=1, replica_groups=mesh['row'=2,'col'=16] {'col'}, dimensions={0}, use_global_device_ids=true | all-gather | bytes 278528 | tf_op jit(solution)/shard_map/all_gather | solution.py:57
  59.9 55.7 %while.40 = (s32[]{:T(128)}, f32[4,8,256]{2,1,0:T(8,128)S(1)}, s32[]{:T(128)}, s32[]{:T(128)}, s32[65]{0:T(128)S(1)}, /*index=5*/s32[65]{0:T(128)S(1)}, f32[32,8...) while((s32[]{:T(128)}, f32[4,8,256]{2,1,0:T(8,128)S(1)}, ...), condition=%wide.region_5.6_spmd, body=%wide.region_3.5_spmd.sunk | while | flops 14687269 | bytes 213307 | solution.py:69
  116.3 22.8 %reduce-scatter.5.cloned.1.call-done = f32[2,8,256]{2,1,0:T(8,128)} async-done(((f32[4,8,256]{2,1,0:T(8,128)}), f32[2,8,256]{2,1,0:T(8,128)}) %reduce-scatter.5.cloned.1.call-update) | async-done | bytes 16400 | tf_op jit(solution)/shard_map/reduce_scatter | solution.py:70
  139.9 22.0 %all_gather.21 = f32[32,8,256]{2,1,0:T(8,128)S(1)} all-gather(f32[2,8,256]{2,1,0:T(8,128)S(1)} %add_subtract_fusion), channel_id=1, replica_groups=mesh['row'=2,'col'=16] {'col'}, dimensions={0}, use_global_device_ids=true | all-gather | bytes 278528 | tf_op jit(solution)/shard_map/all_gather | solution.py:57
  161.9 55.7 %while.41 = (s32[]{:T(128)}, f32[4,8,256]{2,1,0:T(8,128)S(1)}, s32[]{:T(128)}, s32[]{:T(128)}, s32[65]{0:T(128)S(1)}, /*index=5*/s32[65]{0:T(128)S(1)}, f32[32,8...) while((s32[]{:T(128)}, f32[4,8,256]{2,1,0:T(8,128)S(1)}, ...), condition=%wide.region_11.12_spmd, body=%wide.region_9.11_spmd.sunk | while | flops 14687269 | bytes 213307 | solution.py:69
  179.0 0.8 fusion.167
  218.3 20.3 %reduce-scatter.7.cloned.1.call-done = f32[2,8,256]{2,1,0:T(8,128)} async-done(((f32[4,8,256]{2,1,0:T(8,128)}), f32[2,8,256]{2,1,0:T(8,128)}) %reduce-scatter.7.cloned.1.call-update) | async-done | bytes 16400 | tf_op jit(solution)/shard_map/reduce_scatter | solution.py:70
  238.6 0.9 multiply_reduce_fusion.4
  239.5 39.3 %all-reduce.2 = (f32[8]{0:T(128)S(1)}, f32[8]{0:T(128)S(1)}) all-reduce(f32[8]{0:T(128)S(1)} %get-tuple-element.221, f32[8]{0:T(128)S(1)} %get-tuple-element.220), channel_id=1, replica_groups=mesh['row'=2,'col'=16] {'row','col'}, use_global_device_ids=true, to_apply=%region_8.9 | all-reduce | flops 16 | bytes 128 | tf_op jit(solution)/shard_map/psum | solution.py:23
  279.1 40.9 %psum.44 = f32[8]{0:T(128)S(1)} all-reduce(f32[8]{0:T(128)S(1)} %multiply_reduce_fusion.3), channel_id=1, replica_groups=mesh['row'=2,'col'=16] {'row','col'}, use_global_device_ids=true, to_apply=%region_16.17 | all-reduce | flops 8 | bytes 64 | tf_op jit(solution)/shard_map/psum | solution.py:23
  320.1 21.8 %all_gather.22 = f32[32,8,256]{2,1,0:T(8,128)S(1)} all-gather(f32[2,8,256]{2,1,0:T(8,128)S(1)} %multiply_add_fusion.4), channel_id=1, replica_groups=mesh['row'=2,'col'=16] {'col'}, dimensions={0}, use_global_device_ids=true | all-gather | bytes 278528 | tf_op jit(solution)/shard_map/all_gather | solution.py:57
  341.9 55.7 %while.42 = (s32[]{:T(128)}, f32[4,8,256]{2,1,0:T(8,128)S(1)}, s32[]{:T(128)}, s32[]{:T(128)}, s32[65]{0:T(128)S(1)}, /*index=5*/s32[65]{0:T(128)S(1)}, f32[32,8...) while((s32[]{:T(128)}, f32[4,8,256]{2,1,0:T(8,128)S(1)}, ...), condition=%wide.region_19.20_spmd, body=%wide.region_17.19_spmd.sunk | while | flops 14687269 | bytes 213307 | solution.py:69
  398.3 20.3 %reduce-scatter.9.cloned.1.call-done = f32[2,8,256]{2,1,0:T(8,128)} async-done(((f32[4,8,256]{2,1,0:T(8,128)}), f32[2,8,256]{2,1,0:T(8,128)}) %reduce-scatter.9.cloned.1.call-update) | async-done | bytes 16400 | tf_op jit(solution)/shard_map/reduce_scatter | solution.py:70
  418.6 0.9 multiply_reduce_fusion.2
  419.5 39.3 %psum.45 = f32[8]{0:T(128)S(1)} all-reduce(f32[8]{0:T(128)S(1)} %multiply_reduce_fusion.2), channel_id=1, replica_groups=mesh['row'=2,'col'=16] {'row','col'}, use_global_device_ids=true, to_apply=%region_22.23 | all-reduce | flops 8 | bytes 64 | tf_op jit(solution)/shard_map/psum | solution.py:79
  459.0 41.0 %psum.46 = f32[8]{0:T(128)S(1)} all-reduce(f32[8]{0:T(128)S(1)} %get-tuple-element.306), channel_id=1, replica_groups=mesh['row'=2,'col'=16] {'row','col'}, use_global_device_ids=true, to_apply=%region_24.25 | all-reduce | flops 8 | bytes 64 | tf_op jit(solution)/shard_map/psum | solution.py:23
  500.1 21.8 %all_gather.23 = f32[32,8,256]{2,1,0:T(8,128)S(1)} all-gather(f32[2,8,256]{2,1,0:T(8,128)S(1)} %multiply_add_fusion.2), channel_id=1, replica_groups=mesh['row'=2,'col'=16] {'col'}, dimensions={0}, use_global_device_ids=true | all-gather | bytes 278528 | tf_op jit(solution)/shard_map/all_gather | solution.py:57
  521.9 55.7 %while.43 = (s32[]{:T(128)}, f32[4,8,256]{2,1,0:T(8,128)S(1)}, s32[]{:T(128)}, s32[]{:T(128)}, s32[65]{0:T(128)S(1)}, /*index=5*/s32[65]{0:T(128)S(1)}, f32[32,8...) while((s32[]{:T(128)}, f32[4,8,256]{2,1,0:T(8,128)S(1)}, ...), condition=%wide.region_27.28_spmd, body=%wide.region_25.27_spmd.sunk | while | flops 14687269 | bytes 213307 | solution.py:69
  578.3 20.3 %reduce-scatter.11.cloned.1.call-done = f32[2,8,256]{2,1,0:T(8,128)} async-done(((f32[4,8,256]{2,1,0:T(8,128)}), f32[2,8,256]{2,1,0:T(8,128)}) %reduce-scatter.11.cloned.1.call-update) | async-done | bytes 16400 | tf_op jit(solution)/shard_map/reduce_scatter | solution.py:70
  598.6 0.9 multiply_reduce_fusion
  599.5 39.3 %psum.47 = f32[8]{0:T(128)S(1)} all-reduce(f32[8]{0:T(128)S(1)} %multiply_reduce_fusion), channel_id=1, replica_groups=mesh['row'=2,'col'=16] {'row','col'}, use_global_device_ids=true, to_apply=%region_30.31 | all-reduce | flops 8 | bytes 64 | tf_op jit(solution)/shard_map/psum | solution.py:79
  (917 shorter events, 194.2 us)
Async XLA Ops:
  7.2 132.0 %reduce-scatter.5.cloned.1.call-start = ((), (), s32[]{:S(2)}) async-start(), calls=%async_computation.4 | async-start | bytes 49152 | tf_op jit(solution)/shard_map/reduce_scatter | solution.py:70
  12.8 0.7 copy-start.10
  41.3 0.8 copy-start.5
  115.7 0.6 copy-start.1
  115.7 23.5 %copy-start.6 = (f32[2,256]{1,0:T(2,128)S(1)}, f32[2,256]{1,0:T(2,128)}, u32[]{:S(2)}) copy-start(f32[2,256]{1,0:T(2,128)} %param.14) | copy-start | bytes 6148
  115.7 23.5 %copy-start.9 = (f32[2,8,256]{2,1,0:T(8,128)S(1)}, f32[2,8,256]{2,1,0:T(8,128)}, u32[]{:S(2)}) copy-start(f32[2,8,256]{2,1,0:T(8,128)} %param.15) | copy-start | bytes 49156
  116.3 122.3 %reduce-scatter.7.cloned.1.call-start = ((), (), s32[]{:S(2)}) async-start(), calls=%async_computation.5 | async-start | bytes 49152 | tf_op jit(solution)/shard_map/reduce_scatter | solution.py:70
  217.6 0.6 copy-start.2
  218.2 200.4 %reduce-scatter.9.cloned.1.call-start = ((), (), s32[]{:S(2)}) async-start(), calls=%async_computation.6 | async-start | bytes 49152 | tf_op jit(solution)/shard_map/reduce_scatter | solution.py:70
  238.6 40.3 %copy-start.4 = (f32[2,8,256]{2,1,0:T(8,128)S(1)}, f32[2,8,256]{2,1,0:T(8,128)}, u32[]{:S(2)}) copy-start(f32[2,8,256]{2,1,0:T(8,128)} %reduce-scatter.7.cloned.1.call-done) | copy-start | bytes 49156
  397.6 0.6 copy-start.3
  398.3 200.3 %reduce-scatter.11.cloned.1.call-start = ((), (), s32[]{:S(2)}) async-start(), calls=%async_computation.7 | async-start | bytes 49152 | tf_op jit(solution)/shard_map/reduce_scatter | solution.py:70
  418.6 40.2 %copy-start.8 = (f32[2,8,256]{2,1,0:T(8,128)S(1)}, f32[2,8,256]{2,1,0:T(8,128)}, u32[]{:S(2)}) copy-start(f32[2,8,256]{2,1,0:T(8,128)} %reduce-scatter.9.cloned.1.call-done) | copy-start | bytes 49156
  577.6 0.6 copy-start
  598.6 40.2 %copy-start.7 = (f32[2,8,256]{2,1,0:T(8,128)S(1)}, f32[2,8,256]{2,1,0:T(8,128)}, u32[]{:S(2)}) copy-start(f32[2,8,256]{2,1,0:T(8,128)} %reduce-scatter.11.cloned.1.call-done) | copy-start | bytes 49156
Sparse Core Ops, SparseCore 0:
  116.4 22.6 reduce-scatter.4
  218.4 20.1 reduce-scatter.6
  398.4 20.1 reduce-scatter.8
  578.4 20.1 reduce-scatter.10
where the time goes:
time: 649 us; the launch traced here: 646 us
  blocking collectives  311 us (48%)
  local copies, waits for them, and re-layouts  87.6 us (13%)
  waiting for transfers between devices  83.8 us (13%)
  other arithmetic  72.8 us (11%)
  matrix products  39.1 us (6%)
  loops' own time  36.2 us (6%)
  between operations  15.2 us (2%)
    psum x3, blocking collectives, squares(): return lax.psum(jnp.sum(residual * residual, axis=(0, 2)), ('row', 'col'))  121 us
    reduce_scatter x4, waiting for transfers between devices, apply_operator(): lax.psum_scatter(gathered_sum, 'row', scatter_dimension=0, tiled=True)  83.7 us
    all_gather x4, blocking collectives, apply_operator(): pieces = lax.all_gather(vectors, 'col', axis=0, tiled=True)  83.5 us
    psum x2, blocking collectives, shards(): lax.psum(jnp.sum(direction * applied, axis=(0, 2)), ('row', 'col'))  78.6 us
    dot_general x48, matrix products, visit(): jnp.einsum('pab,psa->psb', weights, pieces[local_rows], precision=lax.Pre...  39.1 us
    another operation x4, loops' own time, apply_operator(): gathered_sum = lax.fori_loop(0, turns, visit, empty)  36.2 us
    convert_element_type x48, other arithmetic, group_weights(): inside = (indices < last).astype(jnp.float32)  30.5 us
    scatter-add x48, other arithmetic, visit(): return running.at[cols_group].add(product)  29.3 us
  transfers between devices with their start and end apart: 4, of which 4 were waited for; matrix products, arithmetic and copies ran while one was open for 0% of the time, Pallas kernels for 0%

commit v1 on v0

--- a/solution.py
+++ b/solution.py
@@ -76,7 +76,9 @@
     norm_now = squares(residual)
     for iteration in range(ITERS):
         applied = apply_operator(direction)
-        step_size = norm_now / lax.psum(jnp.sum(direction * applied, axis=(0, 2)), ("row", "col"))
+        step_size = norm_now / lax.psum(
+            lax.psum(jnp.sum(direction * applied, axis=(0, 2)), "row"), "col"
+        )
         solution_field = solution_field + step_size[None, :, None] * direction
         residual = residual - step_size[None, :, None] * applied
         norm_next = squares(residual)

time: 649 us -> 673 us (1.037)
  blocking collectives: 311 us -> 335 us
    psum x2 -> x6, blocking collectives: 78.6 us -> 109 us  [the longest x3 94.3 us: shards(): lax.psum(lax.psum(jnp.sum(direction * applied, axis=(0, 2)), 'row'), 'col')]
where the time goes in v1:
time: 673 us; the launch traced here: 670 us
  blocking collectives  335 us (50%)
  local copies, waits for them, and re-layouts  87.6 us (13%)
  waiting for transfers between devices  84.8 us (13%)
  other arithmetic  72.8 us (11%)
  matrix products  39.2 us (6%)
  loops' own time  36.2 us (5%)
  between operations  15.2 us (2%)
    psum x3, blocking collectives, squares(): return lax.psum(jnp.sum(residual * residual, axis=(0, 2)), ('row', 'col'))  115 us
    psum x3, blocking collectives, shards(): lax.psum(lax.psum(jnp.sum(direction * applied, axis=(0, 2)), 'row'), 'col')  94.3 us
    reduce_scatter x4, waiting for transfers between devices, apply_operator(): lax.psum_scatter(gathered_sum, 'row', scatter_dimension=0, tiled=True)  84.7 us
    all_gather x4, blocking collectives, apply_operator(): pieces = lax.all_gather(vectors, 'col', axis=0, tiled=True)  82.7 us
    dot_general x48, matrix products, visit(): jnp.einsum('pab,psa->psb', weights, pieces[local_rows], precision=lax.Pre...  39.2 us
    another operation x4, loops' own time, apply_operator(): gathered_sum = lax.fori_loop(0, turns, visit, empty)  36.2 us
    convert_element_type x48, other arithmetic, group_weights(): inside = (indices < last).astype(jnp.float32)  30.5 us
    scatter-add x48, other arithmetic, visit(): return running.at[cols_group].add(product)  29.3 us
  transfers between devices with their start and end apart: 4, of which 4 were waited for; matrix products, arithmetic and copies ran while one was open for 0% of the time, Pallas kernels for 0%

profile of v1, /device:TPU:0, one launch (start us, length us, event | category | flops | bytes accessed | tf_op | source)
XLA Modules:
  0.0 670.5 jit_solution(18002674916287197388)
XLA Ops:
  8.0 2.0 sort.17
  13.5 23.5 %all_gather.19 = f32[32,3,256]{2,1,0:T(4,128)S(1)} all-gather(f32[2,3,256]{2,1,0:T(4,128)S(1)} %copy.11), channel_id=1, replica_groups=mesh['row'=2,'col'=16] {'col'}, dimensions={0}, use_global_device_ids=true | all-gather | bytes 104448 | tf_op jit(solution)/shard_map/all_gather | solution.py:27
  36.9 4.3 all_gather.20
  42.1 17.8 %all_gather.18 = f32[32,8,256]{2,1,0:T(8,128)S(1)} all-gather(f32[2,8,256]{2,1,0:T(8,128)S(1)} %copy-done.5), channel_id=1, replica_groups=mesh['row'=2,'col'=16] {'col'}, dimensions={0}, use_global_device_ids=true | all-gather | bytes 278528 | tf_op jit(solution)/shard_map/all_gather | solution.py:57
  59.9 55.7 %while.40 = (s32[]{:T(128)}, f32[4,8,256]{2,1,0:T(8,128)S(1)}, s32[]{:T(128)}, s32[]{:T(128)}, s32[65]{0:T(128)S(1)}, /*index=5*/s32[65]{0:T(128)S(1)}, f32[32,8...) while((s32[]{:T(128)}, f32[4,8,256]{2,1,0:T(8,128)S(1)}, ...), condition=%wide.region_5.6_spmd, body=%wide.region_3.5_spmd.sunk | while | flops 14687269 | bytes 213307 | solution.py:69
  116.3 22.8 %reduce-scatter.5.cloned.1.call-done = f32[2,8,256]{2,1,0:T(8,128)} async-done(((f32[4,8,256]{2,1,0:T(8,128)}), f32[2,8,256]{2,1,0:T(8,128)}) %reduce-scatter.5.cloned.1.call-update) | async-done | bytes 16400 | tf_op jit(solution)/shard_map/reduce_scatter | solution.py:70
  139.9 22.0 %all_gather.21 = f32[32,8,256]{2,1,0:T(8,128)S(1)} all-gather(f32[2,8,256]{2,1,0:T(8,128)S(1)} %add_subtract_fusion), channel_id=1, replica_groups=mesh['row'=2,'col'=16] {'col'}, dimensions={0}, use_global_device_ids=true | all-gather | bytes 278528 | tf_op jit(solution)/shard_map/all_gather | solution.py:57
  161.9 55.7 %while.41 = (s32[]{:T(128)}, f32[4,8,256]{2,1,0:T(8,128)S(1)}, s32[]{:T(128)}, s32[]{:T(128)}, s32[65]{0:T(128)S(1)}, /*index=5*/s32[65]{0:T(128)S(1)}, f32[32,8...) while((s32[]{:T(128)}, f32[4,8,256]{2,1,0:T(8,128)S(1)}, ...), condition=%wide.region_11.12_spmd, body=%wide.region_9.11_spmd.sunk | while | flops 14687269 | bytes 213307 | solution.py:69
  218.3 20.3 %reduce-scatter.7.cloned.1.call-done = f32[2,8,256]{2,1,0:T(8,128)} async-done(((f32[4,8,256]{2,1,0:T(8,128)}), f32[2,8,256]{2,1,0:T(8,128)}) %reduce-scatter.7.cloned.1.call-update) | async-done | bytes 16400 | tf_op jit(solution)/shard_map/reduce_scatter | solution.py:70
  239.5 4.9 psum.64
  244.5 31.4 %psum.65 = f32[8]{0:T(128)S(1)} all-reduce(f32[8]{0:T(128)S(1)} %psum.64), channel_id=1, replica_groups=mesh['row'=2,'col'=16] {'col'}, use_global_device_ids=true, to_apply=%region_15.16 | all-reduce | flops 8 | bytes 64 | tf_op jit(solution)/shard_map/psum | solution.py:79
  275.9 36.8 %psum.63 = f32[8]{0:T(128)S(1)} all-reduce(f32[8]{0:T(128)S(1)} %get-tuple-element.221), channel_id=1, replica_groups=mesh['row'=2,'col'=16] {'row','col'}, use_global_device_ids=true, to_apply=%region_8.9 | all-reduce | flops 8 | bytes 64 | tf_op jit(solution)/shard_map/psum | solution.py:23
  312.9 41.4 %psum.66 = f32[8]{0:T(128)S(1)} all-reduce(f32[8]{0:T(128)S(1)} %multiply_reduce_fusion.3), channel_id=1, replica_groups=mesh['row'=2,'col'=16] {'row','col'}, use_global_device_ids=true, to_apply=%region_17.18 | all-reduce | flops 8 | bytes 64 | tf_op jit(solution)/shard_map/psum | solution.py:23
  354.4 21.1 %all_gather.22 = f32[32,8,256]{2,1,0:T(8,128)S(1)} all-gather(f32[2,8,256]{2,1,0:T(8,128)S(1)} %multiply_add_fusion.4), channel_id=1, replica_groups=mesh['row'=2,'col'=16] {'col'}, dimensions={0}, use_global_device_ids=true | all-gather | bytes 278528 | tf_op jit(solution)/shard_map/all_gather | solution.py:57
  375.4 55.7 %while.42 = (s32[]{:T(128)}, f32[4,8,256]{2,1,0:T(8,128)S(1)}, s32[]{:T(128)}, s32[]{:T(128)}, s32[65]{0:T(128)S(1)}, /*index=5*/s32[65]{0:T(128)S(1)}, f32[32,8...) while((s32[]{:T(128)}, f32[4,8,256]{2,1,0:T(8,128)S(1)}, ...), condition=%wide.region_20.21_spmd, body=%wide.region_18.20_spmd.sunk | while | flops 14687269 | bytes 213307 | solution.py:69
  431.8 21.2 %reduce-scatter.9.cloned.1.call-done = f32[2,8,256]{2,1,0:T(8,128)} async-done(((f32[4,8,256]{2,1,0:T(8,128)}), f32[2,8,256]{2,1,0:T(8,128)}) %reduce-scatter.9.cloned.1.call-update) | async-done | bytes 16400 | tf_op jit(solution)/shard_map/reduce_scatter | solution.py:70
  454.0 4.9 psum.67
  458.9 31.4 %psum.68 = f32[8]{0:T(128)S(1)} all-reduce(f32[8]{0:T(128)S(1)} %psum.67), channel_id=1, replica_groups=mesh['row'=2,'col'=16] {'col'}, use_global_device_ids=true, to_apply=%region_24.25 | all-reduce | flops 8 | bytes 64 | tf_op jit(solution)/shard_map/psum | solution.py:79
  490.5 36.8 %psum.69 = f32[8]{0:T(128)S(1)} all-reduce(f32[8]{0:T(128)S(1)} %get-tuple-element.304), channel_id=1, replica_groups=mesh['row'=2,'col'=16] {'row','col'}, use_global_device_ids=true, to_apply=%region_26.27 | all-reduce | flops 8 | bytes 64 | tf_op jit(solution)/shard_map/psum | solution.py:23
  527.4 21.8 %all_gather.23 = f32[32,8,256]{2,1,0:T(8,128)S(1)} all-gather(f32[2,8,256]{2,1,0:T(8,128)S(1)} %multiply_add_fusion.2), channel_id=1, replica_groups=mesh['row'=2,'col'=16] {'col'}, dimensions={0}, use_global_device_ids=true | all-gather | bytes 278528 | tf_op jit(solution)/shard_map/all_gather | solution.py:57
  549.2 55.7 %while.43 = (s32[]{:T(128)}, f32[4,8,256]{2,1,0:T(8,128)S(1)}, s32[]{:T(128)}, s32[]{:T(128)}, s32[65]{0:T(128)S(1)}, /*index=5*/s32[65]{0:T(128)S(1)}, f32[32,8...) while((s32[]{:T(128)}, f32[4,8,256]{2,1,0:T(8,128)S(1)}, ...), condition=%wide.region_29.30_spmd, body=%wide.region_27.29_spmd.sunk | while | flops 14687269 | bytes 213307 | solution.py:69
  605.6 20.4 %reduce-scatter.11.cloned.1.call-done = f32[2,8,256]{2,1,0:T(8,128)} async-done(((f32[4,8,256]{2,1,0:T(8,128)}), f32[2,8,256]{2,1,0:T(8,128)}) %reduce-scatter.11.cloned.1.call-update) | async-done | bytes 16400 | tf_op jit(solution)/shard_map/reduce_scatter | solution.py:70
  626.9 4.9 psum.70
  631.8 31.4 %psum.71 = f32[8]{0:T(128)S(1)} all-reduce(f32[8]{0:T(128)S(1)} %psum.70), channel_id=1, replica_groups=mesh['row'=2,'col'=16] {'col'}, use_global_device_ids=true, to_apply=%region_33.34 | all-reduce | flops 8 | bytes 64 | tf_op jit(solution)/shard_map/psum | solution.py:79
  (921 shorter events, 197.8 us)
Async XLA Ops:
  7.2 132.0 %reduce-scatter.5.cloned.1.call-start = ((), (), s32[]{:S(2)}) async-start(), calls=%async_computation.4 | async-start | bytes 49152 | tf_op jit(solution)/shard_map/reduce_scatter | solution.py:70
  12.8 0.7 copy-start.10
  41.3 0.8 copy-start.5
  115.7 0.6 copy-start.1
  115.7 23.5 %copy-start.6 = (f32[2,256]{1,0:T(2,128)S(1)}, f32[2,256]{1,0:T(2,128)}, u32[]{:S(2)}) copy-start(f32[2,256]{1,0:T(2,128)} %param.14) | copy-start | bytes 6148
  115.7 23.5 %copy-start.9 = (f32[2,8,256]{2,1,0:T(8,128)S(1)}, f32[2,8,256]{2,1,0:T(8,128)}, u32[]{:S(2)}) copy-start(f32[2,8,256]{2,1,0:T(8,128)} %param.15) | copy-start | bytes 49156
  116.3 122.3 %reduce-scatter.7.cloned.1.call-start = ((), (), s32[]{:S(2)}) async-start(), calls=%async_computation.5 | async-start | bytes 49152 | tf_op jit(solution)/shard_map/reduce_scatter | solution.py:70
  217.6 0.6 copy-start.2
  218.2 234.8 %reduce-scatter.9.cloned.1.call-start = ((), (), s32[]{:S(2)}) async-start(), calls=%async_computation.6 | async-start | bytes 49152 | tf_op jit(solution)/shard_map/reduce_scatter | solution.py:70
  238.6 74.1 %copy-start.4 = (f32[2,8,256]{2,1,0:T(8,128)S(1)}, f32[2,8,256]{2,1,0:T(8,128)}, u32[]{:S(2)}) copy-start(f32[2,8,256]{2,1,0:T(8,128)} %reduce-scatter.7.cloned.1.call-done) | copy-start | bytes 49156
  431.2 0.6 copy-start.3
  431.8 194.2 %reduce-scatter.11.cloned.1.call-start = ((), (), s32[]{:S(2)}) async-start(), calls=%async_computation.7 | async-start | bytes 49152 | tf_op jit(solution)/shard_map/reduce_scatter | solution.py:70
  453.1 37.3 %copy-start.8 = (f32[2,8,256]{2,1,0:T(8,128)S(1)}, f32[2,8,256]{2,1,0:T(8,128)}, u32[]{:S(2)}) copy-start(f32[2,8,256]{2,1,0:T(8,128)} %reduce-scatter.9.cloned.1.call-done) | copy-start | bytes 49156
  604.9 0.6 copy-start
  626.0 37.3 %copy-start.7 = (f32[2,8,256]{2,1,0:T(8,128)S(1)}, f32[2,8,256]{2,1,0:T(8,128)}, u32[]{:S(2)}) copy-start(f32[2,8,256]{2,1,0:T(8,128)} %reduce-scatter.11.cloned.1.call-done) | copy-start | bytes 49156
Sparse Core Ops, SparseCore 0:
  116.4 22.6 reduce-scatter.4
  218.4 20.1 reduce-scatter.6
  431.9 21.0 reduce-scatter.8
  605.7 20.2 reduce-scatter.10
